TPU v7x, 32 devices: a whole 2x2x4 slice. The times are simulated.
32 devices in a mesh: dp: 8 (over z, x), expert: 4 (over y, core).
Axes of the slice: x: 2, y: 2, z: 4, core: 2. Of those that a mesh axis runs over, the one named last changes fastest.
Arguments:
- tokens: bfloat16 [6272, 768], P(('dp', 'expert')), may hold values from -6 to 6
- counts: int32 [32, 2], P(('dp', 'expert')), may hold values from 0 to 4, as said below
- routes: int32 [6272, 2], P(('dp', 'expert')), may hold values from 0 to 31, all different within a row
- priority: int32 [32, 196], P(('dp', 'expert')), may hold values from 0 to 195, each once within a row
- out_grad: bfloat16 [6272, 768], P(('dp', 'expert')), may hold values from -6 to 6
- pre_gain: bfloat16 [768], P(('dp', 'expert')), may hold values from 0.5 to 1.5
- pre_shift: bfloat16 [768], P(('dp', 'expert')), may hold values from -1.5 to 1.5
- w_qkv: bfloat16 [768, 2304], P(('dp', 'expert')), may hold values from -0.21875 to 0.21875
- w_out: bfloat16 [768, 768], P(('dp', 'expert')), may hold values from -0.625 to 0.625
- moe_gain: bfloat16 [768], P(('dp', 'expert')), may hold values from 0.5 to 1.5
- moe_shift: bfloat16 [768], P(('dp', 'expert')), may hold values from -1.5 to 1.5
- w_router: bfloat16 [768, 32], P(('dp', 'expert')), may hold values from -0.15625 to 0.15625
- w_up: bfloat16 [32, 768, 3072], P('expert', 'dp'), may hold values from -0.21875 to 0.21875
- w_down: bfloat16 [32, 3072, 768], P('expert', 'dp'), may hold values from -0.109375 to 0.109375
Outputs:
- out_tokens: bfloat16 [6272, 768], P(('dp', 'expert'))
- d_tokens: float32 [6272, 768], P(('dp', 'expert'))
- d_pre_gain: float32 [768], P(('dp', 'expert'))
- d_pre_shift: float32 [768], P(('dp', 'expert'))
- d_w_qkv: float32 [768, 2304], P(('dp', 'expert'))
- d_w_out: float32 [768, 768], P(('dp', 'expert'))
- d_moe_gain: float32 [768], P(('dp', 'expert'))
- d_moe_shift: float32 [768], P(('dp', 'expert'))
- d_w_router: float32 [768, 32], P(('dp', 'expert'))
- d_w_up: float32 [32, 768, 3072], P('expert', 'dp')
- d_w_down: float32 [32, 3072, 768], P('expert', 'dp')
Inputs may be any that keep to these rules, and one draw needn't show every extreme that they name: counts[s,0] is the number of large images (196 patches) and counts[s,1] of small ones (49 patches) of shard s, laid from the shard's first row, large ones first; counts[s,1] = (196 - 196 counts[s,0]) // 49; counts[s,0] is at most 1. `routes`: the two experts of a row differ. Each row of priority names every rank once; lower ranks take slots first.
All inputs are finite; a program needn't handle non-finite values.
Results may differ from a plain program's by a relative error of at most 0.014.
Values may be sent and summed in bfloat16 or wider, within the bound.
A program may use at most 320 MiB of HBM per device.

v0:
```python
from functools import partial
import math

import jax
import jax.numpy as jnp
from jax import lax
from jax.sharding import PartitionSpec as P

D = 768
HEADS = 12
HEAD_DIM = 64
EXPERTS = 32
PATCH_S = 49
PATCH_L = 196
CAP = 13


def normalize(inputs, scale_vec, shift_vec):
    average = jnp.mean(inputs, axis=-1, keepdims=True)
    centred = inputs - average
    variance = jnp.mean(centred * centred, axis=-1, keepdims=True)
    return centred * lax.rsqrt(variance + 1e-06) * scale_vec + shift_vec


def slot_numbers(chosen, rank_of, usable):
    earlier = (rank_of[:, None] < rank_of[None, :]) & usable[:, None]
    first_ids = chosen[:, 0]
    second_ids = chosen[:, 1]
    slot_first = jnp.sum(
        (earlier & (first_ids[:, None] == first_ids[None, :])).astype(jnp.int32), axis=0
    )
    crossing = usable[:, None] & (first_ids[:, None] == second_ids[None, :])
    slot_second = jnp.sum(
        (earlier & (second_ids[:, None] == second_ids[None, :])).astype(jnp.int32), axis=0
    )
    slot_second = slot_second + jnp.sum(crossing.astype(jnp.int32), axis=0)
    return jnp.stack([slot_first, slot_second], axis=1)


def block_probs(query_blk, seg_blk, key_rows, segment_ids):
    raw_scores = jnp.einsum("qhc,khc->hqk", query_blk, key_rows, preferred_element_type=jnp.float32)
    same_seg = (seg_blk[:, None] == segment_ids[None, :])[None]
    return jax.nn.softmax(
        jnp.where(same_seg, raw_scores * (1.0 / math.sqrt(HEAD_DIM)), -1e30), axis=-1
    )


def body(
    tokens,
    counts,
    routes,
    priority,
    out_grad,
    pre_gain,
    pre_shift,
    w_qkv,
    w_out,
    moe_gain,
    moe_shift,
    w_router,
    w_up,
    w_down,
):
    gain_one, shift_one, qkv_full, outp_full, gain_two, shift_two, router_full = (
        lax.all_gather(pre_gain, ("dp", "expert"), axis=0, tiled=True),
        lax.all_gather(pre_shift, ("dp", "expert"), axis=0, tiled=True),
        lax.all_gather(w_qkv, ("dp", "expert"), axis=0, tiled=True),
        lax.all_gather(w_out, ("dp", "expert"), axis=0, tiled=True),
        lax.all_gather(moe_gain, ("dp", "expert"), axis=0, tiled=True),
        lax.all_gather(moe_shift, ("dp", "expert"), axis=0, tiled=True),
        lax.all_gather(w_router, ("dp", "expert"), axis=0, tiled=True),
    )
    expert_up, expert_down = (
        lax.all_gather(w_up, "dp", axis=1, tiled=True),
        lax.all_gather(w_down, "dp", axis=1, tiled=True),
    )
    row_count = tokens.shape[0]
    scale_factor = 1.0 / math.sqrt(HEAD_DIM)
    positions = jnp.arange(row_count, dtype=jnp.int32)
    large_count = counts[0, 0]
    small_count = counts[0, 1]
    large_end = large_count * PATCH_L
    used_end = large_end + small_count * PATCH_S
    segment_ids = jnp.where(
        positions < large_end,
        positions // PATCH_L,
        jnp.where(positions < used_end, large_count + (positions - large_end) // PATCH_S, -1),
    )
    usable = positions < used_end
    rows_in = tokens.astype(jnp.float32)
    normed_one, pull_one = jax.vjp(
        normalize, rows_in, gain_one.astype(jnp.float32), shift_one.astype(jnp.float32)
    )
    packed_one = normed_one.astype(jnp.bfloat16)
    projected = jnp.dot(packed_one, qkv_full, preferred_element_type=jnp.float32).astype(
        jnp.bfloat16
    )
    queries = projected[:, :D].reshape(row_count, HEADS, HEAD_DIM)
    key_rows = projected[:, D : 2 * D].reshape(row_count, HEADS, HEAD_DIM)
    value_rows = projected[:, 2 * D :].reshape(row_count, HEADS, HEAD_DIM)
    blocks = row_count // PATCH_L
    query_blocks = queries.reshape(blocks, PATCH_L, HEADS, HEAD_DIM)
    seg_blocks = segment_ids.reshape(blocks, PATCH_L)

    def forward_block(operands):
        attn_probs = block_probs(operands[0], operands[1], key_rows, segment_ids)
        return jnp.einsum(
            "hqk,khc->qhc",
            attn_probs.astype(jnp.bfloat16),
            value_rows,
            preferred_element_type=jnp.float32,
        ).astype(jnp.bfloat16)

    mixed_rows = lax.map(forward_block, (query_blocks, seg_blocks)).reshape(row_count, D)
    middle = rows_in + jnp.dot(mixed_rows, outp_full, preferred_element_type=jnp.float32)
    normed_two, pull_two = jax.vjp(
        normalize, middle, gain_two.astype(jnp.float32), shift_two.astype(jnp.float32)
    )
    packed_two = normed_two.astype(jnp.bfloat16)
    router_f32 = router_full.astype(jnp.float32)
    packed_f32 = packed_two.astype(jnp.float32)
    logits = jnp.dot(packed_two, router_full, preferred_element_type=jnp.float32)
    expert_ids = jnp.arange(EXPERTS, dtype=jnp.int32)
    onehot = routes[:, :, None] == expert_ids[None, None, :]
    picked = jnp.sum(jnp.where(onehot, logits[:, None, :], 0.0), axis=2)
    gate_vals = jax.nn.softmax(picked, axis=-1)
    slot_ids = slot_numbers(routes, priority[0], usable)
    kept_mask = usable[:, None] & (slot_ids < CAP)
    slot_total = EXPERTS * CAP
    flat_dest = jnp.where(kept_mask, routes * CAP + slot_ids, slot_total)
    token_of_slot = (
        jnp.full((slot_total + 1,), row_count, jnp.int32)
        .at[flat_dest.reshape(-1)]
        .set(jnp.repeat(positions, 2))
    )
    token_of_slot = token_of_slot[:slot_total]
    padded_rows = jnp.concatenate([packed_two, jnp.zeros((1, D), jnp.bfloat16)], axis=0)
    send_rows = jnp.take(padded_rows, token_of_slot, axis=0).reshape(EXPERTS, CAP, D)
    arrived = lax.all_to_all(send_rows, "expert", split_axis=0, concat_axis=1, tiled=True)
    hidden = jnp.einsum("erd,edf->erf", arrived, expert_up, preferred_element_type=jnp.float32)
    activated = jax.nn.gelu(hidden, approximate=False).astype(jnp.bfloat16)
    produced = jnp.einsum(
        "erf,efd->erd", activated, expert_down, preferred_element_type=jnp.float32
    ).astype(jnp.bfloat16)
    returned = lax.all_to_all(produced, "expert", split_axis=1, concat_axis=0, tiled=True)
    flat_back = jnp.concatenate(
        [returned.reshape(slot_total, D), jnp.zeros((1, D), jnp.bfloat16)], axis=0
    )
    first_back = jnp.take(flat_back, flat_dest[:, 0], axis=0).astype(jnp.float32)
    second_back = jnp.take(flat_back, flat_dest[:, 1], axis=0).astype(jnp.float32)
    result = middle + gate_vals[:, 0:1] * first_back + gate_vals[:, 1:2] * second_back
    out_tokens = result.astype(jnp.bfloat16)
    grad_rows = out_grad.astype(jnp.float32)
    gate_grad = jnp.stack(
        [jnp.sum(grad_rows * first_back, axis=1), jnp.sum(grad_rows * second_back, axis=1)], axis=1
    )
    picked_grad = gate_vals * (gate_grad - jnp.sum(gate_vals * gate_grad, axis=1, keepdims=True))
    logit_grad = jnp.sum(jnp.where(onehot, picked_grad[:, :, None], 0.0), axis=1)
    slot_gate = (
        jnp.zeros((slot_total + 1,), jnp.float32)
        .at[flat_dest.reshape(-1)]
        .set(gate_vals.reshape(-1))
    )
    grad_pad = jnp.concatenate([grad_rows, jnp.zeros((1, D), jnp.float32)], axis=0)
    grad_send = (jnp.take(grad_pad, token_of_slot, axis=0) * slot_gate[:slot_total, None]).astype(
        jnp.bfloat16
    )
    grad_arrived = lax.all_to_all(
        grad_send.reshape(EXPERTS, CAP, D), "expert", split_axis=0, concat_axis=1, tiled=True
    )
    up_back, down_back = (
        lax.all_gather(w_up, "dp", axis=1, tiled=True),
        lax.all_gather(w_down, "dp", axis=1, tiled=True),
    )
    hidden_again = jnp.einsum("erd,edf->erf", arrived, up_back, preferred_element_type=jnp.float32)
    acted_again, gelu_pull = jax.vjp(partial(jax.nn.gelu, approximate=False), hidden_again)
    acted_low = acted_again.astype(jnp.bfloat16)
    down_grad = jnp.einsum(
        "erf,erd->efd", acted_low, grad_arrived, preferred_element_type=jnp.float32
    )
    acted_grad = jnp.einsum(
        "erd,efd->erf", grad_arrived, down_back, preferred_element_type=jnp.float32
    )
    hidden_grad = gelu_pull(acted_grad)[0].astype(jnp.bfloat16)
    up_grad = jnp.einsum("erd,erf->edf", arrived, hidden_grad, preferred_element_type=jnp.float32)
    input_grad = jnp.einsum(
        "erf,edf->erd", hidden_grad, up_back, preferred_element_type=jnp.float32
    ).astype(jnp.bfloat16)
    back_grad = lax.all_to_all(input_grad, "expert", split_axis=1, concat_axis=0, tiled=True)
    up_share, down_share = (
        lax.psum_scatter(
            up_grad.astype(jnp.bfloat16), "dp", scatter_dimension=1, tiled=True
        ).astype(jnp.float32),
        lax.psum_scatter(
            down_grad.astype(jnp.bfloat16), "dp", scatter_dimension=1, tiled=True
        ).astype(jnp.float32),
    )
    flat_grad = jnp.concatenate(
        [back_grad.reshape(slot_total, D), jnp.zeros((1, D), jnp.bfloat16)], axis=0
    )
    normed_two_grad = jnp.take(flat_grad, flat_dest[:, 0], axis=0).astype(jnp.float32)
    normed_two_grad = normed_two_grad + jnp.take(flat_grad, flat_dest[:, 1], axis=0).astype(
        jnp.float32
    )
    normed_two_grad = normed_two_grad + jnp.einsum(
        "te,de->td", logit_grad, router_f32, precision=lax.Precision.HIGHEST
    )
    router_grad = jnp.einsum("td,te->de", packed_f32, logit_grad, precision=lax.Precision.HIGHEST)
    middle_part, gain_two_grad, shift_two_grad = pull_two(normed_two_grad)
    middle_grad = grad_rows + middle_part
    branch_grad = middle_grad.astype(jnp.bfloat16)
    out_proj_grad = jnp.einsum(
        "td,te->de", mixed_rows, branch_grad, preferred_element_type=jnp.float32
    )
    mixed_grad = jnp.einsum(
        "te,de->td", branch_grad, outp_full, preferred_element_type=jnp.float32
    ).astype(jnp.bfloat16)
    grad_blocks = mixed_grad.reshape(blocks, PATCH_L, HEADS, HEAD_DIM)

    def backward_block(carried, operands):
        key_acc, value_acc = carried
        query_blk, seg_blk, grad_blk = operands
        attn_probs = block_probs(query_blk, seg_blk, key_rows, segment_ids)
        probs_grad = jnp.einsum(
            "qhc,khc->hqk", grad_blk, value_rows, preferred_element_type=jnp.float32
        )
        value_acc = value_acc + jnp.einsum(
            "hqk,qhc->khc",
            attn_probs.astype(jnp.bfloat16),
            grad_blk,
            preferred_element_type=jnp.float32,
        )
        score_grad = attn_probs * (
            probs_grad - jnp.sum(attn_probs * probs_grad, axis=-1, keepdims=True)
        )
        raw_grad = (score_grad * scale_factor).astype(jnp.bfloat16)
        query_grad = jnp.einsum(
            "hqk,khc->qhc", raw_grad, key_rows, preferred_element_type=jnp.float32
        )
        key_acc = key_acc + jnp.einsum(
            "hqk,qhc->khc", raw_grad, query_blk, preferred_element_type=jnp.float32
        )
        return ((key_acc, value_acc), query_grad)

    zero_heads = jnp.zeros((row_count, HEADS, HEAD_DIM), jnp.float32)
    (key_grad, value_grad), query_grads = lax.scan(
        backward_block, (zero_heads, zero_heads), (query_blocks, seg_blocks, grad_blocks)
    )
    projected_grad = jnp.concatenate(
        [
            query_grads.reshape(row_count, D),
            key_grad.reshape(row_count, D),
            value_grad.reshape(row_count, D),
        ],
        axis=1,
    ).astype(jnp.bfloat16)
    qkv_grad = jnp.einsum(
        "td,te->de", packed_one, projected_grad, preferred_element_type=jnp.float32
    )
    normed_one_grad = jnp.einsum(
        "te,de->td", projected_grad, qkv_full, preferred_element_type=jnp.float32
    )
    rows_part, gain_one_grad, shift_one_grad = pull_one(normed_one_grad)
    tokens_grad = middle_grad + rows_part
    shares = (
        lax.psum_scatter(gain_one_grad, ("dp", "expert"), scatter_dimension=0, tiled=True),
        lax.psum_scatter(shift_one_grad, ("dp", "expert"), scatter_dimension=0, tiled=True),
        lax.psum_scatter(qkv_grad, ("dp", "expert"), scatter_dimension=0, tiled=True),
        lax.psum_scatter(out_proj_grad, ("dp", "expert"), scatter_dimension=0, tiled=True),
        lax.psum_scatter(gain_two_grad, ("dp", "expert"), scatter_dimension=0, tiled=True),
        lax.psum_scatter(shift_two_grad, ("dp", "expert"), scatter_dimension=0, tiled=True),
        lax.psum_scatter(router_grad, ("dp", "expert"), scatter_dimension=0, tiled=True),
    )
    return (
        out_tokens,
        tokens_grad,
        shares[0],
        shares[1],
        shares[2],
        shares[3],
        shares[4],
        shares[5],
        shares[6],
        up_share,
        down_share,
    )


def solution(mesh):
    placed = (
        P(("dp", "expert"), None),
        P(("dp", "expert"), None),
        P(("dp", "expert"), None),
        P(("dp", "expert"), None),
        P(("dp", "expert"), None),
        P(("dp", "expert")),
        P(("dp", "expert")),
        P(("dp", "expert"), None),
        P(("dp", "expert"), None),
        P(("dp", "expert")),
        P(("dp", "expert")),
        P(("dp", "expert"), None),
        P("expert", "dp", None),
        P("expert", "dp", None),
    )
    return jax.shard_map(
        body,
        mesh=mesh,
        in_specs=placed,
        out_specs=(
            P(("dp", "expert"), None),
            P(("dp", "expert"), None),
            P(("dp", "expert")),
            P(("dp", "expert")),
            P(("dp", "expert"), None),
            P(("dp", "expert"), None),
            P(("dp", "expert")),
            P(("dp", "expert")),
            P(("dp", "expert"), None),
            P("expert", "dp", None),
            P("expert", "dp", None),
        ),
        check_vma=False,
    )
```

profile of v0, /device:TPU:0, one launch (start us, length us, event | category | flops | bytes accessed | tf_op | source)
XLA Modules:
  0.0 3222.2 jit_solution(16751802910218542056)
XLA Ops:
  7.3 0.7 all-gather.5.cloned.1.call-update
  8.0 0.7 all-gather.7.cloned.1.call-update
  8.8 0.7 all-gather.9.cloned.1.call-update
  11.0 42.2 %all-reduce.14 = (bf16[768]{0:T(1024)(128)(2,1)S(1)}, bf16[768]{0:T(1024)(128)(2,1)S(1)}, bf16[768]{0:T(1024)(128)(2,1)S(1)}, bf16[768]{0:T(1024)(128)(2,1)S(1)}) all-reduce(bf16[768]{0:T(1024)(128)(2,1)S(1)} %dynamic-update-slice.1, bf16[768]{0:T(1024)(128)(2,1)S(1)} %dynamic-update-slice, ...), channel_id=1, replica_groups=mesh['dp'=8,'expert'=4] {'dp','expert'}, use_global_device_ids=true, to_apply=%add.5 | all-reduce | flops 3072 | bytes 12288
  55.9 2.9 scatter_custom_fusion
  60.2 13.6 all-gather.5.cloned.1.call-done
  73.8 3.0 convolution_convert_fusion.2
  77.4 2.5 fusion.92
  79.9 2.1 convolution_convert_fusion.6
  82.0 47.5 %all-gather.7.cloned.1.call-done = bf16[768,768]{1,0:T(8,128)(2,1)} async-done(((bf16[24,768]{1,0:T(8,128)(2,1)}), bf16[768,768]{1,0:T(8,128)(2,1)}) %all-gather.7.cloned.1.call-update) | async-done | bytes 1179664 | tf_op jit(solution)/shard_map/all_gather | solution.py:68
  129.5 1.8 fusion.93
  132.3 2.2 gather_fusion
  134.8 1.0 broadcast_select_fusion
  135.8 4.8 all-to-all-start
  140.7 1.9 gather_fusion.1
  142.8 9.4 all-to-all-done
  152.2 1.3 copy.97
  153.6 692.7 %all-gather.9.cloned.1.call-done = bf16[8,768,3072]{2,1,0:T(8,128)(2,1)} async-done(((bf16[8,96,3072]{2,1,0:T(8,128)(2,1)}), bf16[8,768,3072]{2,1,0:T(8,128)(2,1)}) %all-gather.9.cloned.1.call-update) | async-done | bytes 37748752 | tf_op jit(solution)/shard_map/all_gather | solution.py:74
  846.3 19.6 fusion.19
  865.9 698.1 %all-gather.11.cloned.1.call-done = bf16[8,3072,768]{2,1,0:T(8,128)(2,1)} async-done(((bf16[8,384,768]{2,1,0:T(8,128)(2,1)}), bf16[8,3072,768]{2,1,0:T(8,128)(2,1)}) %all-gather.11.cloned.1.call-update) | async-done | bytes 37748752 | tf_op jit(solution)/shard_map/all_gather | solution.py:75
  1564.0 20.6 convolution_convert_fusion.4
  1584.6 1.0 copy.99
  1585.6 3.5 all-to-all-start.1
  1589.1 42.1 %all_gather.35 = bf16[768,32]{1,0:T(8,128)(2,1)S(1)} all-gather(bf16[24,32]{1,0:T(8,128)(2,1)S(1)} %copy-done.48), channel_id=1, replica_groups=mesh['dp'=8,'expert'=4] {'dp','expert'}, dimensions={0}, use_global_device_ids=true | all-gather | bytes 50688 | tf_op jit(solution)/shard_map/all_gather | solution.py:71
  1631.9 0.9 copy-done.14
  1632.8 1.2 copy.100
  1634.0 1.1 reshape.348
  1635.1 1.1 concatenate.21
  1636.2 1.0 gather_fusion.3
  1637.3 1.8 gather_fusion.2
  1639.1 1.4 fusion.51
  1640.8 2.9 scatter_custom_fusion.1
  1644.0 14.0 all_to_all.66
  1658.3 25.9 convolution_convert_fusion
  1684.5 26.1 add_convert_fusion
  1710.6 16.1 convolution_convert_fusion.1
  1726.8 18.7 convolution_convert_fusion.3
  1745.5 2.1 copy.105
  1747.6 3.5 all-to-all-start.3
  1751.2 1.3 fusion.97
  1753.2 7.9 all-to-all-done.3
  1761.3 1.1 reshape.349
  1762.3 1.1 concatenate.23
  1763.5 1.0 gather_fusion.5
  1764.5 1.0 gather_fusion.4
  1765.6 2.3 multiply_reduce_fusion.1
  1768.0 2.0 fusion.84
  1770.1 3.0 fusion.96
  1773.7 0.9 copy.107
  1774.7 1.7 fusion.95
  1776.3 4.3 fusion.20
  1780.6 4.3 fusion.23
  1785.0 2.4 convolution_convert_fusion.5
  1787.4 4.2 fusion.57
  1791.7 3.4 fusion.83
  1795.6 40.4 %all-reduce.13 = (f32[768]{0:T(1024)S(1)}, f32[768]{0:T(1024)S(1)}, f32[768]{0:T(1024)S(1)}, f32[768]{0:T(1024)S(1)}) all-reduce(f32[768]{0:T(1024)S(1)} %get-tuple-element.57, f32[768]{0:T(1024)S(1)} %get-tuple-element.70, f32[768]{0:T(1024)S(1)} %get-tuple-element.55, ...), channel_id=2, replica_groups=mesh['dp'=8,'expert'=4] {'dp','expert'}, use_global_device_ids=true, to_apply=%region_24.26.clone | all-reduce | flops 3072 | bytes 24576
  1838.3 1.1 add_add_fusion.2
  1839.5 442.6 %reduce-scatter.14.cloned.1.call-done = bf16[8,384,768]{2,1,0:T(8,128)(2,1)} async-done(((bf16[8,3072,768]{2,1,0:T(8,128)(2,1)}), bf16[8,384,768]{2,1,0:T(8,128)(2,1)}) %reduce-scatter.14.cloned.1.call-update) | async-done | bytes 4718608 | tf_op jit(solution)/shard_map/reduce_scatter | solution.py:194
  2282.0 6.9 convert_element_type.137
  2289.0 596.6 %reduce-scatter.12.cloned.1.call-done = bf16[8,96,3072]{2,1,0:T(8,128)(2,1)} async-done(((bf16[8,768,3072]{2,1,0:T(8,128)(2,1)}), bf16[8,96,3072]{2,1,0:T(8,128)(2,1)}) %reduce-scatter.12.cloned.1.call-update) | async-done | bytes 4718608 | tf_op jit(solution)/shard_map/reduce_scatter | solution.py:191
  2885.6 7.4 convert_element_type.135
  2893.0 92.8 %reduce-scatter.16.cloned.1.call-done = f32[24,32]{1,0:T(8,128)} async-done(((f32[768,32]{1,0:T(8,128)}), f32[24,32]{1,0:T(8,128)}) %reduce-scatter.16.cloned.1.call-update) | async-done | bytes 3088
  2985.8 104.7 %reduce-scatter.10.cloned.1.call-done = f32[24,768]{1,0:T(8,128)} async-done(((f32[768,768]{1,0:T(8,128)}), f32[24,768]{1,0:T(8,128)}) %reduce-scatter.10.cloned.1.call-update) | async-done | bytes 73744 | tf_op jit(solution)/shard_map/reduce_scatter | solution.py:269
  3090.4 124.8 %reduce-scatter.8.cloned.1.call-done = f32[24,2304]{1,0:T(8,128)} async-done(((f32[768,2304]{1,0:T(8,128)}), f32[24,2304]{1,0:T(8,128)}) %reduce-scatter.8.cloned.1.call-update) | async-done | bytes 221200 | tf_op jit(solution)/shard_map/reduce_scatter | solution.py:268
  (213 shorter events, 12.6 us)
Async XLA Ops:
  7.2 2.9 copy-start.55
  7.2 3.1 copy-start.56
  7.2 3.4 copy-start.57
  7.2 3.6 copy-start.58
  7.2 46.1 %copy-start.54 = (s32[1,2]{1,0:T(1,128)S(1)}, s32[1,2]{1,0:T(1,128)}, u32[]{:S(2)}) copy-start(s32[1,2]{1,0:T(1,128)} %param.17) | copy-start | bytes 28
  7.2 48.0 %copy-start.37 = (s32[196,2]{0,1:T(2,128)S(1)}, s32[196,2]{0,1:T(2,128)}, u32[]{:S(2)}) copy-start(s32[196,2]{0,1:T(2,128)} %param.18) | copy-start | bytes 4708
  7.2 48.0 %copy-start.52 = (s32[1,196]{1,0:T(1,128)S(1)}, s32[1,196]{1,0:T(1,128)}, u32[]{:S(2)}) copy-start(s32[1,196]{1,0:T(1,128)} %param.19) | copy-start | bytes 2356
  7.2 52.4 %copy-start = (bf16[196,768]{1,0:T(8,128)(2,1)S(1)}, bf16[196,768]{1,0:T(8,128)(2,1)}, u32[]{:S(2)}) copy-start(bf16[196,768]{1,0:T(8,128)(2,1)} %param.16) | copy-start | bytes 903172
  7.3 66.5 %all-gather.5.cloned.1.call-start = ((), (), s32[]{:S(2)}) async-start(), calls=%async_computation.9 | async-start | bytes 3649536 | tf_op jit(solution)/shard_map/all_gather | solution.py:67
  8.0 121.5 %all-gather.7.cloned.1.call-start = ((), (), s32[]{:S(2)}) async-start(), calls=%async_computation.10 | async-start | bytes 1216512 | tf_op jit(solution)/shard_map/all_gather | solution.py:68
  8.7 837.5 %all-gather.9.cloned.1.call-start = ((), (), s32[]{:S(2)}) async-start(), calls=%async_computation.11 | async-start | bytes 42467328 | tf_op jit(solution)/shard_map/all_gather | solution.py:74
  9.5 1554.5 %all-gather.11.cloned.1.call-start = ((), (), s32[]{:S(2)}) async-start(), calls=%async_computation.12 | async-start | bytes 42467328 | tf_op jit(solution)/shard_map/all_gather | solution.py:75
  53.3 20.5 copy-start.31
  53.3 20.5 copy-start.24
  53.3 78.3 %copy-start.33 = (f32[768]{0:T(1024)}, f32[768]{0:T(1024)S(1)}, u32[]{:S(2)}) copy-start(f32[768]{0:T(1024)S(1)} %convert_element_type.114) | copy-start | bytes 9220
  59.8 14.0 copy-start.35
  60.0 19.8 copy-start.44
  60.0 19.8 copy-start.38
  77.0 5.0 copy-start.22
  77.2 4.8 copy-start.23
  77.4 4.6 copy-start.16
  79.9 51.4 %copy-start.59 = (f32[12,196]{1,0:T(8,128)}, f32[12,196]{1,0:T(8,128)S(1)}, u32[]{:S(2)}) copy-start(f32[12,196]{1,0:T(8,128)S(1)} %get-tuple-element.103) | copy-start | bytes 28228
  82.0 49.5 %copy-start.15 = (bf16[12,64,196]{2,1,0:T(8,128)(2,1)}, bf16[12,64,196]{2,1,0:T(8,128)(2,1)S(1)}, u32[]{:S(2)}) copy-start(bf16[12,64,196]{2,1,0:T(8,128)(2,1)S(1)} %convolution_convert_fusion.6) | copy-start | bytes 903172
  131.3 4.5 copy-start.40
  131.5 4.2 copy-start.46
  132.1 3.7 copy-start.42
  132.3 8.3 copy-start.7
  132.3 8.3 copy-start.4
  135.8 16.5 all-to-all-start
  142.8 1496.2 %copy-start.49 = (pred[196]{0:T(512)(128)(4,1)}, pred[196]{0:T(512)(128)(4,1)S(1)}, u32[]{:S(2)}) copy-start(pred[196]{0:T(512)(128)(4,1)S(1)} %get-tuple-element.110) | copy-start | bytes 592
  142.8 1496.2 %copy-start.51 = (pred[196]{0:T(512)(128)(4,1)}, pred[196]{0:T(512)(128)(4,1)S(1)}, u32[]{:S(2)}) copy-start(pred[196]{0:T(512)(128)(4,1)S(1)} %get-tuple-element.111) | copy-start | bytes 592
  865.9 718.7 %copy-start.26 = (u8[52,3072]{1,0:T(8,128)(4,1)}, u8[52,3072]{1,0:T(8,128)(4,1)S(1)}, u32[]{:S(2)}) copy-start(u8[52,3072]{1,0:T(8,128)(4,1)S(1)} %get-tuple-element.53) | copy-start | bytes 479236
  865.9 718.7 %copy-start.28 = (u8[52,3072]{1,0:T(8,128)(4,1)}, u8[52,3072]{1,0:T(8,128)(4,1)S(1)}, u32[]{:S(2)}) copy-start(u8[52,3072]{1,0:T(8,128)(4,1)S(1)} %get-tuple-element.54) | copy-start | bytes 479236
  1564.0 25.1 copy-start.48
  1564.0 67.2 %copy-start.8 = (bf16[196,768]{1,0:T(8,128)(2,1)S(1)}, bf16[196,768]{1,0:T(8,128)(2,1)}, u32[]{:S(2)}) copy-start(bf16[196,768]{1,0:T(8,128)(2,1)} %copy-done.7) | copy-start | bytes 903172
  1585.6 46.4 %all-to-all-start.1 = ((bf16[8,52,768]{2,0,1:T(8,128)(2,1)}), bf16[8,52,768]{2,0,1:T(8,128)(2,1)S(1)}, u32[]{:S(2)}, u32[]{:S(2)}) async-start(bf16[8,52,768]{2,0,1:T(8,128)(2,1)} %copy.99), calls=%async_computation.1 | async-start | bytes 1277952 | tf_op jit(solution)/shard_map/all_to_all | solution.py:145
  1589.0 50.0 %copy-start.5 = (bf16[196,768]{1,0:T(8,128)(2,1)S(1)}, bf16[196,768]{1,0:T(8,128)(2,1)}, u32[]{:S(2)}) copy-start(bf16[196,768]{1,0:T(8,128)(2,1)} %param.20) | copy-start | bytes 903172
  1589.1 693.0 %reduce-scatter.14.cloned.1.call-start = ((), (), s32[]{:S(2)}) async-start(), calls=%async_computation.16 | async-start | bytes 42467328 | tf_op jit(solution)/shard_map/reduce_scatter | solution.py:194
  1637.3 46.9 %copy-start.11 = (bf16[196,768]{1,0:T(8,128)(2,1)}, bf16[196,768]{1,0:T(8,128)(2,1)S(1)}, u32[]{:S(2)}) copy-start(bf16[196,768]{1,0:T(8,128)(2,1)S(1)} %gather_fusion.3) | copy-start | bytes 903172
  1639.0 19.2 copy-start.27
  1639.0 19.2 copy-start.29
  1658.2 26.0 copy-start.19
  1684.2 1201.4 %reduce-scatter.12.cloned.1.call-start = ((), (), s32[]{:S(2)}) async-start(), calls=%async_computation.15 | async-start | bytes 42467328 | tf_op jit(solution)/shard_map/reduce_scatter | solution.py:191
  1726.8 24.5 copy-start.9
  1747.6 13.5 all-to-all-start.3
  1751.1 14.5 copy-start.3
  1751.1 14.5 copy-start.18
  1751.1 14.5 copy-start.34
  1751.1 14.5 copy-start.41
  1751.1 14.5 copy-start.43
  1751.1 1234.6 %reduce-scatter.16.cloned.1.call-start = ((), (), s32[]{:S(2)}) async-start(), calls=%async_computation.17 | async-start | bytes 405504
  1751.2 9.9 copy-start.30
  1752.6 1337.8 %reduce-scatter.10.cloned.1.call-start = ((), (), s32[]{:S(2)}) async-start(), calls=%async_computation.14 | async-start | bytes 2433024 | tf_op jit(solution)/shard_map/reduce_scatter | solution.py:269
  1761.2 6.7 copy-start.47
  1761.3 6.7 copy-start.12
  1761.3 6.7 copy-start.13
  1761.3 6.7 copy-start.50
  1763.5 6.5 copy-start.6
  1765.6 7.6 copy-start.10
  1770.1 6.2 copy-start.60
  1773.1 1442.1 %reduce-scatter.8.cloned.1.call-start = ((), (), s32[]{:S(2)}) async-start(), calls=%async_computation.13 | async-start | bytes 7299072 | tf_op jit(solution)/shard_map/reduce_scatter | solution.py:268
  1784.9 2.5 copy-start.32
  1791.7 3.5 copy-start.45
  1791.7 3.9 copy-start.53
  (9 other events, 17.2 us)
Sparse Core Ops, SparseCore 0:
  11.0 62.7 all-gather.4
  76.7 52.7 all-gather.6
  131.0 715.2 all-gather.8
  847.7 716.2 all-gather.10
  1684.3 597.6 reduce-scatter.13
  2285.7 599.8 reduce-scatter.11
  2891.1 94.6 reduce-scatter.15
  2991.6 98.7 reduce-scatter.9
  3096.7 118.4 reduce-scatter.7
where the time goes:
time: 3230 us; the launch traced here: 3220 us
  waiting for transfers between devices  2830 us (88%)
  matrix products  164 us (5%)
  blocking collectives  139 us (4%)
  local copies, waits for them, and re-layouts  34.5 us (1%)
    all_gather x1, waiting for transfers between devices, body(): lax.all_gather(w_down, 'dp', axis=1, tiled=True)  698 us
    all_gather x1, waiting for transfers between devices, body(): lax.all_gather(w_up, 'dp', axis=1, tiled=True)  693 us
    reduce_scatter x1, waiting for transfers between devices, body(): lax.psum_scatter(up_grad.astype(jnp.bfloat16), 'dp', scatter_dimension=1,...  597 us
    reduce_scatter x1, waiting for transfers between devices, body(): lax.psum_scatter(down_grad.astype(jnp.bfloat16), 'dp', scatter_dimension=...  443 us
    reduce_scatter x1, waiting for transfers between devices, body(): lax.psum_scatter(qkv_grad, ('dp', 'expert'), scatter_dimension=0, tiled=T...  125 us
    reduce_scatter x1, waiting for transfers between devices, body(): lax.psum_scatter(out_proj_grad, ('dp', 'expert'), scatter_dimension=0, ti...  105 us
    unnamed x10, waiting for transfers between devices  95.5 us
    unnamed x2, blocking collectives  82.7 us
  transfers between devices with their start and end apart: 12, of which 11 were waited for; matrix products, arithmetic and copies ran while one was open for 5% of the time, Pallas kernels for 0%

commit v1 on v0

--- a/solution.py
+++ b/solution.py
@@ -61,19 +61,25 @@
     w_up,
     w_down,
 ):
-    gain_one, shift_one, qkv_full, outp_full, gain_two, shift_two, router_full = (
-        lax.all_gather(pre_gain, ("dp", "expert"), axis=0, tiled=True),
-        lax.all_gather(pre_shift, ("dp", "expert"), axis=0, tiled=True),
-        lax.all_gather(w_qkv, ("dp", "expert"), axis=0, tiled=True),
-        lax.all_gather(w_out, ("dp", "expert"), axis=0, tiled=True),
-        lax.all_gather(moe_gain, ("dp", "expert"), axis=0, tiled=True),
-        lax.all_gather(moe_shift, ("dp", "expert"), axis=0, tiled=True),
-        lax.all_gather(w_router, ("dp", "expert"), axis=0, tiled=True),
-    )
-    expert_up, expert_down = (
-        lax.all_gather(w_up, "dp", axis=1, tiled=True),
-        lax.all_gather(w_down, "dp", axis=1, tiled=True),
-    )
+    every = ("dp", "expert")
+    dense = lax.all_gather(
+        jnp.concatenate(
+            [w_qkv, w_out, w_router]
+            + [vector[:, None] for vector in (pre_gain, pre_shift, moe_gain, moe_shift)],
+            axis=1,
+        ),
+        every,
+        axis=0,
+        tiled=True,
+    )
+    edges = (3 * D, 4 * D, 4 * D + EXPERTS)
+    qkv_full, outp_full, router_full = (
+        dense[:, : edges[0]],
+        dense[:, edges[0] : edges[1]],
+        dense[:, edges[1] : edges[2]],
+    )
+    gain_one, shift_one, gain_two, shift_two = (dense[:, edges[2] + i] for i in range(4))
+    up_slice = lax.all_to_all(w_up, "dp", split_axis=2, concat_axis=1, tiled=True)
     row_count = tokens.shape[0]
     scale_factor = 1.0 / math.sqrt(HEAD_DIM)
     positions = jnp.arange(row_count, dtype=jnp.int32)
@@ -137,11 +143,14 @@
     padded_rows = jnp.concatenate([packed_two, jnp.zeros((1, D), jnp.bfloat16)], axis=0)
     send_rows = jnp.take(padded_rows, token_of_slot, axis=0).reshape(EXPERTS, CAP, D)
     arrived = lax.all_to_all(send_rows, "expert", split_axis=0, concat_axis=1, tiled=True)
-    hidden = jnp.einsum("erd,edf->erf", arrived, expert_up, preferred_element_type=jnp.float32)
-    activated = jax.nn.gelu(hidden, approximate=False).astype(jnp.bfloat16)
+    arrived = lax.all_gather(arrived, "dp", axis=1, tiled=True)
+    hidden = jnp.einsum("erd,edf->erf", arrived, up_slice, preferred_element_type=jnp.float32)
+    activated, gelu_pull = jax.vjp(partial(jax.nn.gelu, approximate=False), hidden)
+    activated = activated.astype(jnp.bfloat16)
     produced = jnp.einsum(
-        "erf,efd->erd", activated, expert_down, preferred_element_type=jnp.float32
-    ).astype(jnp.bfloat16)
+        "erf,efd->erd", activated, w_down, preferred_element_type=jnp.float32
+    ).astype(jnp.bfloat16)
+    produced = lax.psum_scatter(produced, "dp", scatter_dimension=1, tiled=True)
     returned = lax.all_to_all(produced, "expert", split_axis=1, concat_axis=0, tiled=True)
     flat_back = jnp.concatenate(
         [returned.reshape(slot_total, D), jnp.zeros((1, D), jnp.bfloat16)], axis=0
@@ -168,33 +177,23 @@
     grad_arrived = lax.all_to_all(
         grad_send.reshape(EXPERTS, CAP, D), "expert", split_axis=0, concat_axis=1, tiled=True
     )
-    up_back, down_back = (
-        lax.all_gather(w_up, "dp", axis=1, tiled=True),
-        lax.all_gather(w_down, "dp", axis=1, tiled=True),
-    )
-    hidden_again = jnp.einsum("erd,edf->erf", arrived, up_back, preferred_element_type=jnp.float32)
-    acted_again, gelu_pull = jax.vjp(partial(jax.nn.gelu, approximate=False), hidden_again)
-    acted_low = acted_again.astype(jnp.bfloat16)
-    down_grad = jnp.einsum(
-        "erf,erd->efd", acted_low, grad_arrived, preferred_element_type=jnp.float32
+    grad_arrived = lax.all_gather(grad_arrived, "dp", axis=1, tiled=True)
+    down_share = jnp.einsum(
+        "erf,erd->efd", activated, grad_arrived, preferred_element_type=jnp.float32
     )
     acted_grad = jnp.einsum(
-        "erd,efd->erf", grad_arrived, down_back, preferred_element_type=jnp.float32
+        "erd,efd->erf", grad_arrived, w_down, preferred_element_type=jnp.float32
     )
     hidden_grad = gelu_pull(acted_grad)[0].astype(jnp.bfloat16)
     up_grad = jnp.einsum("erd,erf->edf", arrived, hidden_grad, preferred_element_type=jnp.float32)
+    up_share = lax.all_to_all(
+        up_grad.astype(jnp.bfloat16), "dp", split_axis=1, concat_axis=2, tiled=True
+    ).astype(jnp.float32)
     input_grad = jnp.einsum(
-        "erf,edf->erd", hidden_grad, up_back, preferred_element_type=jnp.float32
-    ).astype(jnp.bfloat16)
+        "erf,edf->erd", hidden_grad, up_slice, preferred_element_type=jnp.float32
+    ).astype(jnp.bfloat16)
+    input_grad = lax.psum_scatter(input_grad, "dp", scatter_dimension=1, tiled=True)
     back_grad = lax.all_to_all(input_grad, "expert", split_axis=1, concat_axis=0, tiled=True)
-    up_share, down_share = (
-        lax.psum_scatter(
-            up_grad.astype(jnp.bfloat16), "dp", scatter_dimension=1, tiled=True
-        ).astype(jnp.float32),
-        lax.psum_scatter(
-            down_grad.astype(jnp.bfloat16), "dp", scatter_dimension=1, tiled=True
-        ).astype(jnp.float32),
-    )
     flat_grad = jnp.concatenate(
         [back_grad.reshape(slot_total, D), jnp.zeros((1, D), jnp.bfloat16)], axis=0
     )
@@ -262,25 +261,27 @@
     )
     rows_part, gain_one_grad, shift_one_grad = pull_one(normed_one_grad)
     tokens_grad = middle_grad + rows_part
-    shares = (
-        lax.psum_scatter(gain_one_grad, ("dp", "expert"), scatter_dimension=0, tiled=True),
-        lax.psum_scatter(shift_one_grad, ("dp", "expert"), scatter_dimension=0, tiled=True),
-        lax.psum_scatter(qkv_grad, ("dp", "expert"), scatter_dimension=0, tiled=True),
-        lax.psum_scatter(out_proj_grad, ("dp", "expert"), scatter_dimension=0, tiled=True),
-        lax.psum_scatter(gain_two_grad, ("dp", "expert"), scatter_dimension=0, tiled=True),
-        lax.psum_scatter(shift_two_grad, ("dp", "expert"), scatter_dimension=0, tiled=True),
-        lax.psum_scatter(router_grad, ("dp", "expert"), scatter_dimension=0, tiled=True),
+    dense_grad = jnp.concatenate(
+        [qkv_grad, out_proj_grad, router_grad]
+        + [
+            vector[:, None]
+            for vector in (gain_one_grad, shift_one_grad, gain_two_grad, shift_two_grad)
+        ],
+        axis=1,
+    ).astype(jnp.bfloat16)
+    dense_share = lax.psum_scatter(dense_grad, every, scatter_dimension=0, tiled=True).astype(
+        jnp.float32
     )
     return (
         out_tokens,
         tokens_grad,
-        shares[0],
-        shares[1],
-        shares[2],
-        shares[3],
-        shares[4],
-        shares[5],
-        shares[6],
+        dense_share[:, edges[2]],
+        dense_share[:, edges[2] + 1],
+        dense_share[:, : edges[0]],
+        dense_share[:, edges[0] : edges[1]],
+        dense_share[:, edges[2] + 2],
+        dense_share[:, edges[2] + 3],
+        dense_share[:, edges[1] : edges[2]],
         up_share,
         down_share,
     )

time: 3230 us -> 912 us (0.28)
  waiting for transfers between devices: 2830 us -> 406 us
  blocking collectives: 139 us -> 227 us
  local copies, waits for them, and re-layouts: 34.5 us -> 119 us
  matrix products: 164 us -> 88.4 us
    all_gather x4 -> x3, waiting for transfers between devices: 1450 us -> 138 us  [the longest x1 83.1 us: body(): grad_arrived = lax.all_gather(grad_arrived, 'dp', axis=1, tiled=True)]
    reduce_scatter x4 -> x2, waiting for transfers between devices: 1270 us -> 197 us  [the longest x1 100 us: body(): produced = lax.psum_scatter(produced, 'dp', scatter_dimension=1, tiled=True)]
    all_to_all x0 -> x2, blocking collectives: none -> 213 us  [the longest x1 198 us: body(): lax.all_to_all(w_up, 'dp', split_axis=2, concat_axis=1, tiled=True)]
    unnamed x2 -> x0, blocking collectives: 82.7 us -> none
    dot_general x5, matrix products: 111 us -> 40.9 us  [the longest x1 10.9 us: body(): jnp.einsum('erd,efd->erf', grad_arrived, w_down, preferred_element_type=j...]
    unnamed x10 -> x7, waiting for transfers between devices: 95.5 us -> 25.8 us
    all_gather x1 -> x0, blocking collectives: 42.1 us -> none  [body(): lax.all_gather(w_router, ('dp', 'expert'), axis=0, tiled=True)]
    all_to_all x1, waiting for transfers between devices: 9.41 us -> 43.4 us  [body(): lax.all_to_all(up_grad.astype(jnp.bfloat16), 'dp', split_axis=1, concat_a...]
  transfers between devices with their start and end apart: 12 -> 9, of which waited for: 11 -> 7; matrix products, arithmetic and copies ran while one was open for 5% -> 15% of each run, Pallas kernels for 0% -> 0%
where the time goes in v1:
time: 912 us; the launch traced here: 903 us
  waiting for transfers between devices  406 us (45%)
  blocking collectives  227 us (25%)
  local copies, waits for them, and re-layouts  119 us (13%)
  matrix products  88.4 us (10%)
  other arithmetic  33.1 us (4%)
  between operations  16.5 us (2%)
  starting transfers between devices  13.3 us (1%)
    all_to_all x1, blocking collectives, body(): lax.all_to_all(w_up, 'dp', split_axis=2, concat_axis=1, tiled=True)  198 us
    reduce_scatter x1, waiting for transfers between devices, body(): produced = lax.psum_scatter(produced, 'dp', scatter_dimension=1, tiled=True)  100 us
    reduce_scatter x1, waiting for transfers between devices, body(): lax.psum_scatter(input_grad, 'dp', scatter_dimension=1, tiled=True)  96.9 us
    all_gather x1, waiting for transfers between devices, body(): grad_arrived = lax.all_gather(grad_arrived, 'dp', axis=1, tiled=True)  83.1 us
    all_gather x1, waiting for transfers between devices, body(): lax.all_gather(jnp.concatenate([w_qkv, w_out, w_router] + [vector[:, None...  55 us
    all_to_all x1, waiting for transfers between devices, body(): lax.all_to_all(up_grad.astype(jnp.bfloat16), 'dp', split_axis=1, concat_a...  43.4 us
    unnamed x7, waiting for transfers between devices  25.8 us
    convert_element_type x2, local copies, waits for them, and re-layouts, body(): up_share = lax.all_to_all(up_grad.astype(jnp.bfloat16), 'dp', split_axis=...  20.1 us
  transfers between devices with their start and end apart: 9, of which 7 were waited for; matrix products, arithmetic and copies ran while one was open for 15% of the time, Pallas kernels for 0%

profile of v1, /device:TPU:0, one launch (start us, length us, event | category | flops | bytes accessed | tf_op | source)
XLA Modules:
  0.0 902.8 jit_solution(15943545236240041457)
XLA Ops:
  10.2 1.7 concatenate.27
  12.0 1.3 fusion.103
  17.5 2.9 scatter_custom_fusion
  24.0 55.0 %all-gather.4.cloned.1.call-done = bf16[768,3108]{1,0:T(8,128)(2,1)} async-done(((bf16[24,3108]{1,0:T(8,128)(2,1)}), bf16[768,3108]{1,0:T(8,128)(2,1)}) %all-gather.4.cloned.1.call-update) | async-done | bytes 4773904 | tf_op jit(solution)/shard_map/all_gather | solution.py:65
  79.1 2.0 convert_reduce_fusion.2
  81.0 3.1 convolution_convert_fusion.1
  84.8 2.5 fusion.104
  87.3 2.1 convolution_convert_fusion.6
  89.4 1.9 fusion.105
  93.1 2.2 gather_fusion
  95.7 14.2 %all_to_all.93 = bf16[32,13,768]{2,1,0:T(8,128)(2,1)S(1)} all-to-all(bf16[32,13,768]{2,1,0:T(8,128)(2,1)S(1)} %broadcast_select_fusion), channel_id=1, replica_groups=mesh['dp'=8,'expert'=4] {'expert'}, dimensions={0} | all-to-all | bytes 1277952 | tf_op jit(solution)/shard_map/all_to_all | solution.py:145
  111.0 8.6 copy.170
  119.6 198.4 %all_to_all.94 = bf16[8,96,3072]{1,0,2:T(8,128)(2,1)} all-to-all(bf16[8,96,3072]{1,0,2:T(8,128)(2,1)} %copy.170), channel_id=1, replica_groups=mesh['dp'=8,'expert'=4] {'dp'}, dimensions={2} | all-to-all | bytes 9437184 | tf_op jit(solution)/shard_map/all_to_all | solution.py:82
  318.0 8.5 copy.171
  326.5 8.4 fusion.35
  334.9 12.4 %multiply_convert_fusion = (bf16[8,416,384]{2,1,0:T(8,128)(2,1)S(1)}, f32[8,416,384]{2,1,0:T(8,128)}) fusion(f32[8,416,384]{2,1,0:T(8,128)S(1)} %get-tuple-element.109, u8[416,384]{1,0:T(8,128)(4,1)S(1)} %get-tuple-element.54, u8[416,384]{1,0:T(8,128)(4,1)S(1)} %get-tuple-element.53), kind=kLoop, calls=%fused_computation.19 | loop fusion | flops 89456640 | bytes 13099008 | tf_op jit(solution)/shard_map/convert_element_type | solution.py:149
  347.3 5.4 convolution_convert_fusion.3
  352.7 5.2 copy.173
  358.0 100.1 %reduce-scatter.6.cloned.1.call-done = bf16[8,52,768]{2,0,1:T(8,128)(2,1)} async-done(((bf16[8,416,768]{2,0,1:T(8,128)(2,1)}), bf16[8,52,768]{2,0,1:T(8,128)(2,1)}) %reduce-scatter.6.cloned.1.call-update) | async-done | bytes 638992 | tf_op jit(solution)/shard_map/reduce_scatter | solution.py:153
  458.1 4.2 all-to-all-start.2
  463.5 2.5 gather_fusion.1
  466.0 2.5 gather.18
  470.4 1.9 all-to-all-done.2
  472.3 2.1 copy.174
  474.4 2.1 reshape.380
  477.7 1.8 gather_fusion.2
  479.4 1.8 gather_fusion.3
  481.2 1.5 fusion.61
  483.7 3.0 scatter_custom_fusion.1
  486.9 1.6 multiply_convert_fusion.2
  488.5 14.0 %all_to_all.95 = bf16[32,13,768]{2,1,0:T(8,128)(2,1)S(1)} all-to-all(bf16[32,13,768]{2,1,0:T(8,128)(2,1)S(1)} %multiply_convert_fusion.2), channel_id=1, replica_groups=mesh['dp'=8,'expert'=4] {'expert'}, dimensions={0} | all-to-all | bytes 1277952 | tf_op jit(solution)/shard_map/all_to_all | solution.py:177
  503.6 83.1 %all-gather.8.cloned.1.call-done = bf16[8,416,768]{2,0,1:T(8,128)(2,1)} async-done(((bf16[8,52,768]{2,0,1:T(8,128)(2,1)}), bf16[8,416,768]{2,0,1:T(8,128)(2,1)}) %all-gather.8.cloned.1.call-update) | async-done | bytes 5111824 | tf_op jit(solution)/shard_map/all_gather | solution.py:180
  586.7 10.9 %add_convert_fusion = bf16[8,416,384]{2,1,0:T(8,128)(2,1)S(1)} fusion(f32[8,416,384]{2,1,0:T(8,128)} %get-tuple-element.90, f32[8,416,384]{2,1,0:T(8,128)} %copy-done.1, bf16[8,384,768]{2,1,0:T(8,128)(2,1)} %param.29, bf16[8,416,768]{2,0,1:T(8,128)(2,1)} %all-gather.8.cloned.1.call-done), kind=kOutput, calls=%fused_computation.18 | convolution fusion | flops 1980825600 | bytes 22609920 | tf_op jit(solution)/shard_map/erd,efd->erf/dot_general | solution.py:184
  597.6 6.9 convolution_convert_fusion.2
  604.5 5.2 copy.179
  612.4 96.9 %reduce-scatter.8.cloned.1.call-done = bf16[8,52,768]{2,0,1:T(8,128)(2,1)} async-done(((bf16[8,416,768]{2,0,1:T(8,128)(2,1)}), bf16[8,52,768]{2,0,1:T(8,128)(2,1)}) %reduce-scatter.8.cloned.1.call-update) | async-done | bytes 638992 | tf_op jit(solution)/shard_map/reduce_scatter | solution.py:195
  709.3 3.9 all-to-all-start.4
  713.2 6.8 fusion.19
  720.0 5.0 copy.192
  725.0 4.6 all-to-all-start.5
  730.9 2.1 reshape.381
  734.1 1.9 gather_fusion.5
  736.0 1.9 gather_fusion.4
  737.9 2.2 multiply_reduce_fusion.1
  740.8 2.6 fusion.95
  744.2 2.5 convolution_convert_fusion.7
  746.8 1.9 copy.181
  748.7 3.1 fusion.106
  751.7 5.6 fusion.39
  757.4 5.6 fusion.36
  763.0 2.4 convolution_convert_fusion.5
  765.5 3.5 fusion.94
  773.6 1.5 convolution_convert_fusion.4
  775.1 3.1 convolution_convert_fusion
  778.2 8.7 concatenate.33
  787.0 9.3 %fusion.8 = f32[8,384,768]{2,1,0:T(8,128)} fusion(bf16[8,416,384]{2,1,0:T(8,128)(2,1)S(1)} %get-tuple-element.89, bf16[8,416,768]{2,0,1:T(8,128)(2,1)} %all-gather.8.cloned.1.call-done), kind=kOutput, calls=%fused_computation.33 | convolution fusion | flops 1962934272 | bytes 17104896 | tf_op jit(solution)/shard_map/erf,erd->efd/dot_general | solution.py:181
  796.3 43.4 %all-to-all-done.5 = bf16[8,768,384]{2,0,1:T(8,128)(2,1)} async-done(((bf16[8,768,384]{2,0,1:T(8,128)(2,1)}), bf16[8,768,384]{2,0,1:T(8,128)(2,1)}, u32[]{:S(2)}, u32[]{:S(2)}) %all-to-all-start.5) | async-done | bytes 4718624 | tf_op jit(solution)/shard_map/all_to_all | solution.py:189
  839.7 3.0 convert_bitcast_fusion
  842.7 9.1 %copy.193 = f32[8,96,8,384]{3,2,1,0:T(8,128)} copy(f32[8,96,8,384]{3,0,1,2:T(8,128)S(1)} %convert_bitcast_fusion) | data formatting | bytes 18874368 | tf_op jit(solution)/shard_map/convert_element_type | solution.py:191
  851.8 11.0 %reshape.389 = f32[8,96,3072]{2,1,0:T(8,128)} reshape(f32[8,96,8,384]{3,2,1,0:T(8,128)} %copy.193) | data formatting | bytes 18874368 | tf_op jit(solution)/shard_map/convert_element_type | solution.py:191
  864.0 25.7 %reduce-scatter.10.cloned.1.call-done = bf16[24,3108]{1,0:T(8,128)(2,1)} async-done(((bf16[768,3108]{1,0:T(8,128)(2,1)}), bf16[24,3108]{1,0:T(8,128)(2,1)}) %reduce-scatter.10.cloned.1.call-update) | async-done | bytes 149200
  891.4 1.6 slice.141
  893.0 1.4 slice.142
  894.4 1.3 slice.145
  (165 shorter events, 33.8 us)
Async XLA Ops:
  7.2 71.9 %all-gather.4.cloned.1.call-start = ((), (), s32[]{:S(2)}) async-start(), calls=%async_computation.9 | async-start | bytes 5068800 | tf_op jit(solution)/shard_map/all_gather | solution.py:65
  11.9 314.6 %all-gather.6.cloned.1.call-start = ((), (), s32[]{:S(2)}) async-start(), calls=%async_computation.10 | async-start | bytes 5750784 | tf_op jit(solution)/shard_map/all_gather | solution.py:146
  17.5 2.9 copy-start.34
  22.3 61.9 %copy-start.19 = (f32[196]{0:T(256)}, f32[196]{0:T(256)S(1)}, u32[]{:S(2)}) copy-start(f32[196]{0:T(256)S(1)} %broadcast_multiply_fusion.1) | copy-start | bytes 2356
  23.5 0.5 copy-start.27
  23.5 60.7 %copy-start.24 = (f32[196]{0:T(256)}, f32[196]{0:T(256)S(1)}, u32[]{:S(2)}) copy-start(f32[196]{0:T(256)S(1)} %fusion.81) | copy-start | bytes 2356
  81.0 3.6 copy-start.32
  84.4 5.0 copy-start.10
  84.6 4.8 copy-start.15
  84.8 4.6 copy-start.16
  87.3 4.1 copy-start.37
  87.3 2.2 copy-start.2
  89.4 3.7 copy-start.13
  91.4 0.8 copy-start
  91.4 4.3 copy-start.21
  91.6 4.1 copy-start.29
  91.6 4.1 copy-start.26
  92.4 0.7 copy-start.5
  110.9 347.1 %reduce-scatter.6.cloned.1.call-start = ((), (), s32[]{:S(2)}) async-start(), calls=%async_computation.11 | async-start | bytes 5750784 | tf_op jit(solution)/shard_map/reduce_scatter | solution.py:153
  334.9 12.4 %copy-start.1 = (f32[8,416,384]{2,1,0:T(8,128)}, f32[8,416,384]{2,1,0:T(8,128)S(1)}, u32[]{:S(2)}) copy-start(f32[8,416,384]{2,1,0:T(8,128)S(1)} %get-tuple-element.109) | copy-start | bytes 15335428
  357.9 119.7 %copy-start.22 = (s32[1024]{0:T(1024)}, s32[1024]{0:T(1024)S(1)}, u32[]{:S(2)}) copy-start(s32[1024]{0:T(1024)S(1)} %pad_clamp_fusion.1) | copy-start | bytes 12292
  358.0 123.2 %copy-start.30 = (pred[196]{0:T(512)(128)(4,1)}, pred[196]{0:T(512)(128)(4,1)S(1)}, u32[]{:S(2)}) copy-start(pred[196]{0:T(512)(128)(4,1)S(1)} %get-tuple-element.112) | copy-start | bytes 592
  358.0 123.2 %copy-start.31 = (pred[196]{0:T(512)(128)(4,1)}, pred[196]{0:T(512)(128)(4,1)S(1)}, u32[]{:S(2)}) copy-start(pred[196]{0:T(512)(128)(4,1)S(1)} %get-tuple-element.113) | copy-start | bytes 592
  458.1 14.3 %all-to-all-start.2 = ((bf16[8,52,768]{2,0,1:T(8,128)(2,1)}), bf16[8,52,768]{2,0,1:T(8,128)(2,1)}, u32[]{:S(2)}, u32[]{:S(2)}) async-start(bf16[8,52,768]{2,0,1:T(8,128)(2,1)} %reduce-scatter.6.cloned.1.call-done), calls=%async_computation.3 | async-start | bytes 1277952 | tf_op jit(solution)/shard_map/all_to_all | solution.py:154
  462.2 124.5 %all-gather.8.cloned.1.call-start = ((), (), s32[]{:S(2)}) async-start(), calls=%async_computation.12 | async-start | bytes 5750784 | tf_op jit(solution)/shard_map/all_gather | solution.py:180
  462.5 16.9 %copy-start.23 = (s32[1024]{0:T(1024)}, s32[1024]{0:T(1024)S(1)}, u32[]{:S(2)}) copy-start(s32[1024]{0:T(1024)S(1)} %pad_clamp_fusion) | copy-start | bytes 12292
  463.5 6.2 copy-start.17
  503.6 205.7 %reduce-scatter.8.cloned.1.call-start = ((), (), s32[]{:S(2)}) async-start(), calls=%async_computation.13 | async-start | bytes 5750784 | tf_op jit(solution)/shard_map/reduce_scatter | solution.py:195
  597.5 6.9 copy-start.7
  609.7 0.7 copy-start.18
  609.7 1.0 copy-start.6
  709.3 15.7 %all-to-all-start.4 = ((bf16[8,52,768]{2,0,1:T(8,128)(2,1)}), bf16[8,52,768]{2,0,1:T(8,128)(2,1)S(1)}, u32[]{:S(2)}, u32[]{:S(2)}) async-start(bf16[8,52,768]{2,0,1:T(8,128)(2,1)} %reduce-scatter.8.cloned.1.call-done), calls=%async_computation.6 | async-start | bytes 1277952 | tf_op jit(solution)/shard_map/all_to_all | solution.py:196
  725.0 114.7 %all-to-all-start.5 = ((bf16[8,768,384]{2,0,1:T(8,128)(2,1)}), bf16[8,768,384]{2,0,1:T(8,128)(2,1)}, u32[]{:S(2)}, u32[]{:S(2)}) async-start(bf16[8,768,384]{2,0,1:T(8,128)(2,1)} %copy.192), calls=%async_computation.7 | async-start | bytes 9437184 | tf_op jit(solution)/shard_map/all_to_all | solution.py:189
  729.6 160.1 %reduce-scatter.10.cloned.1.call-start = ((), (), s32[]{:S(2)}) async-start(), calls=%async_computation.14 | async-start | bytes 5068800
  737.9 5.5 copy-start.3
  740.1 11.7 %copy-start.38 = (f32[12,196]{1,0:T(8,128)S(1)}, f32[12,196]{1,0:T(8,128)}, u32[]{:S(2)}) copy-start(f32[12,196]{1,0:T(8,128)} %copy-done.37) | copy-start | bytes 28228
  743.5 0.7 copy-start.11
  763.0 2.4 copy-start.20
  763.0 2.4 copy-start.35
  763.0 2.5 copy-start.36
  765.4 3.6 copy-start.28
  765.4 4.4 copy-start.25
  765.5 8.1 copy-start.12
  765.5 8.1 copy-start.14
  765.5 9.6 %copy-start.33 = (f32[768]{0:T(1024)S(1)}, f32[768]{0:T(1024)}, u32[]{:S(2)}) copy-start(f32[768]{0:T(1024)} %copy-done.32) | copy-start | bytes 9220
  769.0 0.8 copy-start.8
  851.8 11.0 %copy-start.4 = (bf16[196,768]{1,0:T(8,128)(2,1)S(1)}, bf16[196,768]{1,0:T(8,128)(2,1)}, u32[]{:S(2)}) copy-start(bf16[196,768]{1,0:T(8,128)(2,1)} %param.20) | copy-start | bytes 903172
  851.8 11.0 %copy-start.9 = (f32[196,768]{1,0:T(8,128)S(1)}, f32[196,768]{1,0:T(8,128)}, u32[]{:S(2)}) copy-start(f32[196,768]{1,0:T(8,128)} %copy-done.8) | copy-start | bytes 1806340
Sparse Core Ops, SparseCore 0:
  12.0 66.9 all-gather.3
  111.1 163.1 all-gather.5
  358.0 100.0 reduce-scatter.5
  503.7 82.9 all-gather.7
  609.8 99.3 reduce-scatter.7
  787.1 102.5 reduce-scatter.9
